TPU v7x, 32 devices: a whole 2x2x4 slice. The times are simulated.
32 devices in a mesh: ctx: 8 (over z, core), inner: 4 (over y, x).
Axes of the slice: x: 2, y: 2, z: 4, core: 2. Of those that a mesh axis runs over, the one named last changes fastest.
Arguments:
- tokens: bfloat16 [4096, 2048], P(('ctx', 'inner')), may hold values from -6 to 6
- project_weight: bfloat16 [2048, 2, 4096], P('ctx', None, 'inner'), may hold values from -0.125 to 0.125
- state_weight: bfloat16 [2048, 2, 512], P('ctx', None, 'inner'), may hold values from -0.125 to 0.125
- step_weight: bfloat16 [2048, 64], P('ctx', 'inner'), may hold values from -0.125 to 0.125
- mixer_taps: float32 [5, 4096], P(None, 'inner'), may hold values from -2.5 to 2.5
- state_taps: float32 [5, 2, 512], replicated, may hold values from -2.5 to 2.5
- step_bias: float32 [64], P('inner'), may hold values from -4.6 to -2.3
- decay_log: float32 [64], P('inner'), may hold values from -13 to 0.5, as said below
- norm_gain: float32 [4096], replicated, may hold values from 0.1 to 1.9
Outputs:
- mixed_output: bfloat16 [4096, 4096], P(('ctx', 'inner'))
Inputs may be any that keep to these rules, and one draw needn't show every extreme that they name: `decay_log`: one value a head.
All inputs are finite; a program needn't handle non-finite values.
Results may differ from a plain program's by a relative error of at most 0.0075.
Values may be sent and summed in bfloat16 or wider, within the bound.
No kernel may reach another device: no remote copies, remote signals or barrier semaphores. Data moves between devices by JAX's collectives and lax.ppermute only.
A program may use at most 64 MiB of HBM per device.

v0:
```python
import jax
import jax.numpy as jnp
from jax import lax
from jax.sharding import PartitionSpec as P

H = 64
P_SIZE = 64
N = 128
G = 4
CONV = 4
SPAN = 128
EPSILON = 1e-05


def passed_along(x, axis, by):
    count = lax.axis_size(axis)
    pairs = [(i, i + by) for i in range(count) if 0 <= i + by < count]
    return lax.ppermute(x, axis, pairs)


def entering(x, axis, join, neutral):
    place = lax.axis_index(axis)
    gathered = jax.tree.map(
        lambda a, kind: lax.all_gather(a.astype(kind), axis), x, (jnp.bfloat16, jnp.bfloat16)
    )
    state = jax.tree.map(lambda a, e: jnp.zeros_like(a) + jnp.asarray(e, a.dtype), x, neutral)

    def one(turn, state):
        return join(
            state,
            jax.tree.map(
                lambda a, own: lax.dynamic_index_in_dim(a, turn, 0, False).astype(own.dtype),
                gathered,
                x,
            ),
        )

    return lax.fori_loop(0, place, one, state)


def partner(value, axis, stride):
    mask = 2**stride
    pairs = [(source, source ^ mask) for source in range(lax.axis_size(axis))]
    return lax.ppermute(value, axis, pairs)


def conv_apply(taps, previous, current):
    extended = jnp.concatenate([previous, current], axis=0)
    length_rows = current.shape[0]
    mixed = jnp.broadcast_to(taps[CONV], current.shape)
    for offset in range(CONV):
        mixed = mixed + taps[offset] * extended[offset : offset + length_rows].astype(jnp.float32)
    return jax.nn.silu(mixed).astype(jnp.bfloat16)


def join_chain(earlier, later):
    return (earlier[0] + later[0], jnp.exp(later[0])[:, None, None] * earlier[1] + later[1])


def carry_block(state, inputs):
    decay_sum, added = inputs
    return (jnp.exp(decay_sum)[:, None, None] * state + added, state)


def pick_group(values, group):
    shaped = values.reshape(values.shape[:-1] + (N, G))
    return lax.dynamic_index_in_dim(shaped, group, shaped.ndim - 1, keepdims=False)


def on_device(
    tokens,
    project_weight,
    state_weight,
    step_weight,
    mixer_taps,
    state_taps,
    step_bias,
    decay_log,
    norm_gain,
):
    inner_id = lax.axis_index("inner")
    project_rows, state_rows, step_rows = (
        lax.all_gather(project_weight, "ctx", axis=0, tiled=True),
        lax.all_gather(state_weight, "ctx", axis=0, tiled=True),
        lax.all_gather(step_weight, "ctx", axis=0, tiled=True),
    )
    heads_here = step_weight.shape[1]
    width_here = project_weight.shape[2]
    model_width = project_rows.shape[0]
    group = inner_id * heads_here // (H // G)
    slice_cols = state_weight.shape[2]
    state_conv = lax.dynamic_slice_in_dim(state_taps, inner_id * slice_cols, slice_cols, 2)
    joined = jnp.concatenate(
        [
            project_rows.reshape(model_width, 2 * width_here),
            state_rows.reshape(model_width, 2 * slice_cols),
            step_rows,
        ],
        axis=1,
    )
    projected = jnp.dot(
        lax.all_gather(tokens, "inner", axis=0, tiled=True),
        joined,
        preferred_element_type=jnp.float32,
    ).astype(jnp.bfloat16)
    rows_total = projected.shape[0]
    gate_values = projected[:, :width_here]
    x_pre = projected[:, width_here : 2 * width_here]
    state_pre = projected[:, 2 * width_here : 2 * width_here + 2 * slice_cols].reshape(
        rows_total, 2, slice_cols
    )
    step_raw = projected[:, 2 * width_here + 2 * slice_cols :]
    edge_row = rows_total - (CONV - 1)
    prior_x, prior_state = passed_along((x_pre[edge_row:], state_pre[edge_row:]), "ctx", 1)
    x_vals = conv_apply(mixer_taps, prior_x, x_pre)
    state_vals = conv_apply(state_conv, prior_state, state_pre)
    state_all = lax.all_gather(state_vals, "inner", axis=2, tiled=True)
    state_vals = pick_group(state_all, group)
    blocks = rows_total // SPAN
    b_blocks = state_vals[:, 0].reshape(blocks, SPAN, N)
    c_blocks = state_vals[:, 1].reshape(blocks, SPAN, N)
    step_size = jax.nn.softplus(step_raw.astype(jnp.float32) + step_bias)
    step_heads = step_size.T.reshape(heads_here, blocks, SPAN)
    cumul = jnp.cumsum(step_heads * (-jnp.exp(decay_log))[:, None, None], axis=2)
    scores = jnp.einsum("ctn,csn->cts", c_blocks, b_blocks, preferred_element_type=jnp.float32)
    lower = jnp.tril(jnp.ones((SPAN, SPAN), dtype=bool))
    spacing = jnp.where(lower, cumul[..., :, None] - cumul[..., None, :], -jnp.inf)
    mixing = (scores[None] * jnp.exp(spacing) * step_heads[:, :, None, :]).astype(jnp.bfloat16)
    x_blocks = x_vals.reshape(blocks, SPAN, heads_here, P_SIZE)
    diagonal = jnp.einsum("hcts,cshp->cthp", mixing, x_blocks, preferred_element_type=jnp.float32)
    ending = cumul[:, :, -1]
    to_end = jnp.exp(ending[..., None] - cumul) * step_heads
    weighted_b = (b_blocks.astype(jnp.float32)[None] * to_end[..., None]).astype(jnp.bfloat16)
    fresh = jnp.einsum("hcsn,cshp->chnp", weighted_b, x_blocks, preferred_element_type=jnp.float32)
    empty_state = jnp.zeros((heads_here, N, P_SIZE), jnp.float32)
    block_state, local_in = lax.scan(carry_block, empty_state, (ending.T, fresh))
    block_log = jnp.sum(ending, axis=1)
    before_log = (jnp.cumsum(ending, axis=1) - ending).T
    _, prior_block = entering(
        (block_log, block_state), "ctx", join_chain, (jnp.zeros_like(block_log), empty_state)
    )
    state_in = local_in + jnp.exp(before_log)[:, :, None, None] * prior_block[None]
    c_scaled = (c_blocks.astype(jnp.float32)[None] * jnp.exp(cumul)[..., None]).astype(jnp.bfloat16)
    state_high = state_in.astype(jnp.bfloat16)
    state_low = (state_in - state_high.astype(jnp.float32)).astype(jnp.bfloat16)
    offdiag = jnp.einsum(
        "hctn,chnp->cthp", c_scaled, state_high, preferred_element_type=jnp.float32
    )
    offdiag = offdiag + jnp.einsum(
        "hctn,chnp->cthp", c_scaled, state_low, preferred_element_type=jnp.float32
    )
    outputs = (diagonal + offdiag).reshape(rows_total, width_here)
    gated = (outputs * jax.nn.silu(gate_values.astype(jnp.float32))).astype(jnp.bfloat16)
    gated_wide = gated.astype(jnp.float32)
    squares = jnp.sum(gated_wide * gated_wide, axis=1)
    group_devices = H // G // heads_here
    for bit in range(group_devices.bit_length() - 1):
        squares = squares + partner(squares, "inner", bit)
    power = squares[:, None] / (H * P_SIZE // G)
    gain_here = lax.dynamic_slice_in_dim(norm_gain, inner_id * width_here, width_here, 0)
    normed = (gated_wide * lax.rsqrt(power + EPSILON) * gain_here).astype(jnp.bfloat16)
    result = lax.all_to_all(normed, "inner", split_axis=0, concat_axis=1, tiled=True)
    return result


def solution(mesh):
    placed = (
        P(("ctx", "inner"), None),
        P("ctx", None, "inner"),
        P("ctx", None, "inner"),
        P("ctx", "inner"),
        P(None, "inner"),
        P(),
        P("inner"),
        P("inner"),
        P(),
    )
    return jax.shard_map(
        on_device, mesh=mesh, in_specs=placed, out_specs=P(("ctx", "inner"), None), check_vma=False
    )
```

profile of v0, /device:TPU:25, one launch (start us, length us, event | category | flops | bytes accessed | tf_op | source)
XLA Modules:
  0.0 290.0 jit_solution(8972189394626062334)
XLA Ops:
  8.8 14.7 %all_gather.27 = bf16[2048,16]{0,1:T(8,128)(2,1)S(1)} all-gather(bf16[256,16]{0,1:T(8,128)(2,1)} %param.16), channel_id=1, replica_groups=mesh['ctx'=8,'inner'=4] {'ctx'}, dimensions={0}, use_global_device_ids=true | all-gather | bytes 73728 | tf_op jit(solution)/shard_map/all_gather | solution.py:85
  24.5 6.7 %all-gather.10.cloned.1.call-done = bf16[2048,2,128]{2,1,0:T(2,128)(2,1)} async-done(((bf16[256,2,128]{2,1,0:T(2,128)(2,1)}), bf16[2048,2,128]{2,1,0:T(2,128)(2,1)}) %all-gather.10.cloned.1.call-update) | async-done | bytes 1048592 | tf_op jit(solution)/shard_map/all_gather | solution.py:84
  32.6 80.6 %all-gather.8.cloned.1.call-done = bf16[2048,2,1024]{2,1,0:T(2,128)(2,1)} async-done(((bf16[256,2,1024]{2,1,0:T(2,128)(2,1)}), bf16[2048,2,1024]{2,1,0:T(2,128)(2,1)}) %all-gather.8.cloned.1.call-update) | async-done | bytes 8388624 | tf_op jit(solution)/shard_map/all_gather | solution.py:83
  113.2 10.2 %copy.119 = bf16[256,8,2,1024]{3,1,2,0:T(8,128)(2,1)} copy(bf16[256,8,2,1024]{3,2,1,0:T(2,128)(2,1)} %bitcast.91) | data formatting | bytes 16777216
  123.3 27.6 %all-gather.12.cloned.1.call-done = bf16[512,2048]{1,0:T(8,128)(2,1)} async-done(((bf16[128,2048]{1,0:T(8,128)(2,1)}), bf16[512,2048]{1,0:T(8,128)(2,1)}) %all-gather.12.cloned.1.call-update) | async-done | bytes 2097168 | tf_op jit(solution)/shard_map/all_gather | solution.py:102
  150.9 9.8 %fusion.11 = bf16[512,2320]{0,1:T(8,128)(2,1)S(1)} fusion(bf16[512,2048]{1,0:T(8,128)(2,1)} %all-gather.12.cloned.1.call-done, bf16[2048,16]{1,0:T(8,128)(2,1)} %copy.91, bf16[2048,256]{1,0:T(8,128)(2,1)S(1)} %bitcast.100, bf16[2048,2048]{1,0:T(8,128)(2,1)} %bitcast.92), kind=kOutput, calls=%fused_computation.20 | convolution fusion | flops 4895088640 | bytes 13975552 | tf_op jit(solution)/shard_map/dot_general | solution.py:101
  163.7 1.8 copy.94
  165.5 2.5 multiply_convert_fusion.10
  168.0 1.8 copy.96
  170.8 1.5 collective-permute-start
  174.0 1.6 collective-permute-done
  175.5 3.8 %multiply_convert_fusion.7 = bf16[512,1024]{0,1:T(8,128)(2,1)S(1)} fusion(bf16[512,1024]{0,1:T(8,128)(2,1)S(1)} %slice.107, bf16[3,1024]{0,1:T(8,128)(2,1)} %collective-permute-done, f32[1024]{0:T(1024)S(1)} %bitcast.112, f32[1024]{0:T(1024)S(1)} %bitcast.113, f32[1024]{0:T(1024)S(1)} %bitcast.110, f32[1024]{0:T(1024)S(1)} %bitcast.111, f32[1024]{0:T(1024)S(1)} %bitcast.109), kind=kLoop, calls=%fused_computation.53 | loop fusion | flops 13631488 | bytes 2123776 | tf_op jit(solution)/shard_map/convert_element_type | solution.py:53
  179.6 17.8 %all-gather.14.cloned.1.call-done = bf16[512,2,512]{0,1,2:T(2,128)(2,1)} async-done(((bf16[512,2,128]{0,1,2:T(2,128)(2,1)}), bf16[512,2,512]{0,1,2:T(2,128)(2,1)}) %all-gather.14.cloned.1.call-update) | async-done | bytes 1048592 | tf_op jit(solution)/shard_map/all_gather | solution.py:117
  198.9 4.0 %fusion.26 = f32[4,16,128,64]{3,2,1,0:T(8,128)} fusion(f32[16,4,128]{2,0,1:T(8,128)S(1)} %get-tuple-element.170, f32[4,128,128]{2,1,0:T(8,128)S(1)} %convert_element_type.129, bf16[4,128,16,64]{1,0,3,2:T(4,128)(2,1)S(1)} %reshape.90), kind=kOutput, calls=%fused_computation.36 | convolution fusion | flops 136314880 | bytes 3440640 | tf_op jit(solution)/shard_map/hcsn,cshp->chnp/dot_general | solution.py:134
  202.8 10.1 %while.26 = (s32[]{:T(128)}, f32[16,128,64]{2,1,0:T(8,128)S(1)}, f32[4,16,128,64]{3,2,1,0:T(8,128)}, f32[4,16]{1,0:T(4,128)S(1)}, f32[4,16,128,64]{3,2,1,0:T(8,128)}, /*index=5*/s32[]{:T(128)}, s32[]{:T(128)}) while((s32[]{:T(128)}, f32[16,128,64]{2,1,0:T(8,128)S(1)}, f32[4,16,128,64]{3,2,1,0:T(8,128)}, f32[4,16]{1,0:T(4,128)S(1)}, ...), condition=%wide.region_2.3_spmd.clone, body=%wide.region_1.2_spmd.clone.sunk | while | flops 524291 | bytes 3146528 | solution.py:136
  203.9 1.4 bitcast_add_fusion.2
  215.4 13.6 %all-reduce = bf16[128]{0:T(256)(128)(2,1)S(1)} all-reduce(bf16[128]{0:T(256)(128)(2,1)S(1)} %dynamic-update-slice), channel_id=2, replica_groups=mesh['ctx'=8,'inner'=4] {'ctx'}, use_global_device_ids=true, to_apply=%add | all-reduce | flops 128 | bytes 512
  230.2 3.3 %fusion.18 = f32[4,16,64,128]{3,2,1,0:T(8,128)} fusion(f32[16,4,128]{2,0,1:T(8,128)S(1)} %copy_bitcast_fusion.2, f32[16,4,128]{2,0,1:T(8,128)S(1)} %reduce_window_sum.22, f32[4,128,128]{2,1,0:T(8,128)S(1)} %fusion.65, pred[128,128]{1,0:T(8,128)(4,1)S(1)} %iota_compare_fusion, bf16[4,128,16,64]{1,0,3,2:T(4,128)(2,1)S(1)} %reshape.90), kind=kOutput, calls=%fused_computation.28 | convolution fusion | flops 139460608 | bytes 3489792 | tf_op jit(solution)/shard_map/hcts,cshp->cthp/dot_general | solution.py:130
  233.6 8.9 %all-gather.16.cloned.1.call-done = bf16[128,128,64]{1,2,0:T(8,128)(2,1)} async-done(((bf16[16,128,64]{1,2,0:T(8,128)(2,1)}), bf16[128,128,64]{1,2,0:T(8,128)(2,1)}) %all-gather.16.cloned.1.call-update) | async-done | bytes 2097168 | tf_op jit(solution)/shard_map/all_gather | solution.py:24
  242.5 11.0 %while.25 = (s32[]{:T(128)}, f32[16,128,64]{2,1,0:T(8,128)S(1)}, s32[]{:T(128)}, bf16[8,16]{1,0:T(8,128)(2,1)S(1)}, bf16[8,16,128,64]{2,3,1,0:T(8,128)(2,1)}, /*index=5*/s32[]{:T(128)}, s32[]{:T(128)}, s32[]{:T(128)}) while((s32[]{:T(128)}, f32[16,128,64]{2,1,0:T(8,128)S(1)}, s32[]{:T(128)}, bf16[8,16]{1,0:T(8,128)(2,1)S(1)}, ...), condition=%wide.region_6.7_spmd, body=%wide.region_5.6_spmd.sunk | while | flops 393237 | bytes 2359583 | solution.py:38
  253.5 5.2 %fusion.15 = f32[4,16,64,128]{3,2,1,0:T(8,128)S(1)} fusion(f32[4,16,128,64]{3,2,1,0:T(8,128)} %get-tuple-element.77, f32[16,4,128]{2,0,1:T(8,128)S(1)} %get-tuple-element.169, f32[4,128,128]{2,1,0:T(8,128)S(1)} %convert_element_type.135, f32[16,128,64]{2,1,0:T(8,128)S(1)} %get-tuple-element.79, f32[4,16]{1,0:T(4,128)S(1)} %exponential_bitcast_fusion.1), kind=kOutput, calls=%fused_computation.22 | convolution fusion | flops 139460608 | bytes 5013760 | tf_op jit(solution)/shard_map/hctn,chnp->cthp/dot_general | solution.py:149
  258.8 2.7 add_bitcast_fusion
  262.9 2.0 fusion.23
  265.3 16.9 %all_to_all.19 = bf16[4,128,1024]{1,2,0:T(8,128)(2,1)S(1)} all-to-all(bf16[4,128,1024]{1,2,0:T(8,128)(2,1)S(1)} %copy_bitcast_fusion.1), channel_id=1, replica_groups=mesh['ctx'=8,'inner'=4] {'inner'}, dimensions={0} | all-to-all | bytes 2097152 | tf_op jit(solution)/shard_map/all_to_all | solution.py:162
  (104 shorter events, 37.2 us)
Async XLA Ops:
  6.5 24.7 %all-gather.10.cloned.1.call-start = ((), (), s32[]{:S(2)}) async-start(), calls=%async_computation.2 | async-start | bytes 1179648 | tf_op jit(solution)/shard_map/all_gather | solution.py:84
  7.3 105.9 %all-gather.8.cloned.1.call-start = ((), (), s32[]{:S(2)}) async-start(), calls=%async_computation.1 | async-start | bytes 9437184 | tf_op jit(solution)/shard_map/all_gather | solution.py:83
  8.0 142.9 %all-gather.12.cloned.1.call-start = ((), (), s32[]{:S(2)}) async-start(), calls=%async_computation.3 | async-start | bytes 2621440 | tf_op jit(solution)/shard_map/all_gather | solution.py:102
  8.7 188.7 %all-gather.14.cloned.1.call-start = ((), (), s32[]{:S(2)}) async-start(), calls=%async_computation.4 | async-start | bytes 1310720 | tf_op jit(solution)/shard_map/all_gather | solution.py:117
  160.7 13.2 %copy-start.1 = (bf16[512,2320]{0,1:T(8,128)(2,1)}, bf16[512,2320]{0,1:T(8,128)(2,1)S(1)}, u32[]{:S(2)}) copy-start(bf16[512,2320]{0,1:T(8,128)(2,1)S(1)} %fusion.11) | copy-start | bytes 7127044
  160.7 9.2 %copy-start.5 = (f32[16]{0:T(128)S(1)}, f32[16]{0:T(128)}, u32[]{:S(2)}) copy-start(f32[16]{0:T(128)} %param.20) | copy-start | bytes 196
  160.8 9.2 %copy-start.3 = (f32[5,1024]{1,0:T(8,128)S(1)}, f32[5,1024]{1,0:T(8,128)}, u32[]{:S(2)}) copy-start(f32[5,1024]{1,0:T(8,128)} %param.17) | copy-start | bytes 61444
  160.8 11.5 %copy-start.4 = (f32[16]{0:T(128)S(1)}, f32[16]{0:T(128)}, u32[]{:S(2)}) copy-start(f32[16]{0:T(128)} %param.19) | copy-start | bytes 196
  161.0 4.6 %collective-permute-start.1 = (bf16[3,2,128]{2,0,1:T(4,128)(2,1)S(1)}, bf16[3,2,128]{2,0,1:T(4,128)(2,1)S(1)}, u32[]{:S(2)}, u32[]{:S(2)}) collective-permute-start(bf16[3,2,128]{2,0,1:T(4,128)(2,1)S(1)} %copy.93), channel_id=1, source_target_pairs={{0,4},{4,8},{8,12},{12,16},{16,20},{20,24},{24,28},{1,5},{5,9},{9,... | collective-permute-start | bytes 4616 | tf_op jit(solution)/shard_map/ppermute | solution.py:18
  169.9 72.6 %all-gather.16.cloned.1.call-start = ((), (), s32[]{:S(2)}) async-start(), calls=%async_computation.5 | async-start | bytes 2359296 | tf_op jit(solution)/shard_map/all_gather | solution.py:24
  170.8 4.7 %collective-permute-start = (bf16[3,1024]{0,1:T(8,128)(2,1)}, bf16[3,1024]{0,1:T(8,128)(2,1)}, u32[]{:S(2)}, u32[]{:S(2)}) collective-permute-start(bf16[3,1024]{0,1:T(8,128)(2,1)} %slice.106), channel_id=1, source_target_pairs={{0,4},{4,8},{8,12},{12,16},{16,20},{20,24},{24,28},{1,5},{5,9},{9,... | collective-permute-start | bytes 18440 | tf_op jit(solution)/shard_map/ppermute | solution.py:18
  202.8 11.1 %copy-start.6 = (u32[32]{0:T(128)S(1)}, u32[32]{0:T(128)}, u32[]{:S(2)}) copy-start(u32[32]{0:T(128)} %constant.96) | copy-start | bytes 388
  253.5 5.3 %copy-start = (f32[4,16,128,64]{3,2,1,0:T(8,128)S(1)}, f32[4,16,128,64]{3,2,1,0:T(8,128)}, u32[]{:S(2)}) copy-start(f32[4,16,128,64]{3,2,1,0:T(8,128)} %get-tuple-element.77) | copy-start | bytes 6291460
  253.5 5.3 %copy-start.2 = (f32[4,16,64,128]{3,2,1,0:T(8,128)S(1)}, f32[4,16,64,128]{3,2,1,0:T(8,128)}, u32[]{:S(2)}) copy-start(f32[4,16,64,128]{3,2,1,0:T(8,128)} %fusion.18) | copy-start | bytes 6291460
  262.9 2.0 dynamic-slice-start
Sparse Core Ops, SparseCore 0:
  8.9 22.2 all-gather.9
  32.8 80.3 all-gather.7
  115.0 35.8 all-gather.11
  170.0 27.4 all-gather.13
  214.0 28.3 all-gather.15
where the time goes:
time: 291 us; the launch traced here: 290 us
  waiting for transfers between devices  145 us (50%)
  blocking collectives  45.3 us (16%)
  local copies, waits for them, and re-layouts  33.9 us (12%)
  matrix products  25.2 us (9%)
  other arithmetic  22.9 us (8%)
  between operations  14.1 us (5%)
  starting transfers between devices  2.92 us (1%)
    all_gather x1, waiting for transfers between devices, on_device(): lax.all_gather(project_weight, 'ctx', axis=0, tiled=True)  80.6 us
    all_gather x1, waiting for transfers between devices, on_device(): lax.all_gather(tokens, 'inner', axis=0, tiled=True)  27.6 us
    all_gather x1, waiting for transfers between devices, on_device(): state_all = lax.all_gather(state_vals, 'inner', axis=2, tiled=True)  17.8 us
    all_to_all x1, blocking collectives, on_device(): lax.all_to_all(normed, 'inner', split_axis=0, concat_axis=1, tiled=True)  16.9 us
    all_gather x1, blocking collectives, on_device(): lax.all_gather(step_weight, 'ctx', axis=0, tiled=True)  14.7 us
    unnamed x1, blocking collectives  13.6 us
    unnamed x19, local copies, waits for them, and re-layouts  12.4 us
    dot_general x1, matrix products, on_device(): jnp.dot(lax.all_gather(tokens, 'inner', axis=0, tiled=True), joined, pref...  9.82 us
  transfers between devices with their start and end apart: 7, of which 6 were waited for; matrix products, arithmetic and copies ran while one was open for 10% of the time, Pallas kernels for 0%

commit v1 on v0

--- a/solution.py
+++ b/solution.py
@@ -114,7 +114,7 @@
     prior_x, prior_state = passed_along((x_pre[edge_row:], state_pre[edge_row:]), "ctx", 1)
     x_vals = conv_apply(mixer_taps, prior_x, x_pre)
     state_vals = conv_apply(state_conv, prior_state, state_pre)
-    state_all = lax.all_gather(state_vals, "inner", axis=2, tiled=True)
+    state_all = jnp.concatenate(lax.all_gather(state_vals, "inner"), axis=2)
     state_vals = pick_group(state_all, group)
     blocks = rows_total // SPAN
     b_blocks = state_vals[:, 0].reshape(blocks, SPAN, N)

time: 291 us -> 291 us (level)
  no operation moved by 1% of the time
where the time goes in v1:
time: 291 us; the launch traced here: 290 us
  waiting for transfers between devices  145 us (50%)
  blocking collectives  45.3 us (16%)
  local copies, waits for them, and re-layouts  33.6 us (12%)
  matrix products  25.2 us (9%)
  other arithmetic  22.9 us (8%)
  between operations  14.1 us (5%)
  starting transfers between devices  2.92 us (1%)
    all_gather x1, waiting for transfers between devices, on_device(): lax.all_gather(project_weight, 'ctx', axis=0, tiled=True)  80.6 us
    all_gather x1, waiting for transfers between devices, on_device(): lax.all_gather(tokens, 'inner', axis=0, tiled=True)  27.6 us
    all_gather x1, waiting for transfers between devices, on_device(): state_all = jnp.concatenate(lax.all_gather(state_vals, 'inner'), axis=2)  17.8 us
    all_to_all x1, blocking collectives, on_device(): lax.all_to_all(normed, 'inner', split_axis=0, concat_axis=1, tiled=True)  16.9 us
    all_gather x1, blocking collectives, on_device(): lax.all_gather(step_weight, 'ctx', axis=0, tiled=True)  14.7 us
    unnamed x1, blocking collectives  13.7 us
    unnamed x19, local copies, waits for them, and re-layouts  12.4 us
    dot_general x1, matrix products, on_device(): jnp.dot(lax.all_gather(tokens, 'inner', axis=0, tiled=True), joined, pref...  9.82 us
  transfers between devices with their start and end apart: 7, of which 6 were waited for; matrix products, arithmetic and copies ran while one was open for 10% of the time, Pallas kernels for 0%

profile of v1, /device:TPU:25, one launch (start us, length us, event | category | flops | bytes accessed | tf_op | source)
XLA Modules:
  0.0 289.8 jit_solution(12553801805903941235)
XLA Ops:
  8.8 14.7 %all_gather.30 = bf16[2048,16]{0,1:T(8,128)(2,1)S(1)} all-gather(bf16[256,16]{0,1:T(8,128)(2,1)} %param.16), channel_id=1, replica_groups=mesh['ctx'=8,'inner'=4] {'ctx'}, dimensions={0}, use_global_device_ids=true | all-gather | bytes 73728 | tf_op jit(solution)/shard_map/all_gather | solution.py:85
  24.5 6.7 %all-gather.11.cloned.1.call-done = bf16[2048,2,128]{2,1,0:T(2,128)(2,1)} async-done(((bf16[256,2,128]{2,1,0:T(2,128)(2,1)}), bf16[2048,2,128]{2,1,0:T(2,128)(2,1)}) %all-gather.11.cloned.1.call-update) | async-done | bytes 1048592 | tf_op jit(solution)/shard_map/all_gather | solution.py:84
  32.6 80.6 %all-gather.9.cloned.1.call-done = bf16[2048,2,1024]{2,1,0:T(2,128)(2,1)} async-done(((bf16[256,2,1024]{2,1,0:T(2,128)(2,1)}), bf16[2048,2,1024]{2,1,0:T(2,128)(2,1)}) %all-gather.9.cloned.1.call-update) | async-done | bytes 8388624 | tf_op jit(solution)/shard_map/all_gather | solution.py:83
  113.2 10.2 %copy.88 = bf16[256,8,2,1024]{3,1,2,0:T(8,128)(2,1)} copy(bf16[256,8,2,1024]{3,2,1,0:T(2,128)(2,1)} %bitcast.94) | data formatting | bytes 16777216
  123.3 27.6 %all-gather.13.cloned.1.call-done = bf16[512,2048]{1,0:T(8,128)(2,1)} async-done(((bf16[128,2048]{1,0:T(8,128)(2,1)}), bf16[512,2048]{1,0:T(8,128)(2,1)}) %all-gather.13.cloned.1.call-update) | async-done | bytes 2097168 | tf_op jit(solution)/shard_map/all_gather | solution.py:102
  150.9 9.8 %fusion.11 = bf16[512,2320]{0,1:T(8,128)(2,1)S(1)} fusion(bf16[512,2048]{1,0:T(8,128)(2,1)} %all-gather.13.cloned.1.call-done, bf16[2048,16]{1,0:T(8,128)(2,1)} %copy.63, bf16[2048,256]{1,0:T(8,128)(2,1)S(1)} %bitcast.105, bf16[2048,2048]{1,0:T(8,128)(2,1)} %bitcast.95), kind=kOutput, calls=%fused_computation.20 | convolution fusion | flops 4895088640 | bytes 13975552 | tf_op jit(solution)/shard_map/dot_general | solution.py:101
  163.7 1.8 copy.65
  165.5 2.5 multiply_convert_fusion.10
  169.0 1.5 collective-permute-start
  172.1 1.6 collective-permute-done
  173.7 3.8 %multiply_convert_fusion.7 = bf16[512,1024]{0,1:T(8,128)(2,1)S(1)} fusion(bf16[512,1024]{0,1:T(8,128)(2,1)S(1)} %slice.107, bf16[3,1024]{0,1:T(8,128)(2,1)} %collective-permute-done, f32[1024]{0:T(1024)S(1)} %bitcast.116, f32[1024]{0:T(1024)S(1)} %bitcast.117, f32[1024]{0:T(1024)S(1)} %bitcast.114, f32[1024]{0:T(1024)S(1)} %bitcast.115, f32[1024]{0:T(1024)S(1)} %bitcast.113), kind=kLoop, calls=%fused_computation.53 | loop fusion | flops 13631488 | bytes 2123776 | tf_op jit(solution)/shard_map/convert_element_type | solution.py:53
  177.8 17.8 %all-gather.15.cloned.1.call-done = bf16[2048,2,128]{2,0,1:T(8,128)(2,1)} async-done(((bf16[512,2,128]{2,0,1:T(8,128)(2,1)}), bf16[2048,2,128]{2,0,1:T(8,128)(2,1)}) %all-gather.15.cloned.1.call-update) | async-done | bytes 1048592 | tf_op jit(solution)/shard_map/all_gather | solution.py:117
  195.6 2.5 copy.67
  198.6 4.0 %fusion.26 = f32[4,16,128,64]{3,2,1,0:T(8,128)} fusion(f32[16,4,128]{2,0,1:T(8,128)S(1)} %get-tuple-element.155, f32[4,128,128]{2,1,0:T(8,128)S(1)} %convert_element_type.129, bf16[4,128,16,64]{1,0,3,2:T(4,128)(2,1)S(1)} %reshape.90), kind=kOutput, calls=%fused_computation.36 | convolution fusion | flops 136314880 | bytes 3440640 | tf_op jit(solution)/shard_map/hcsn,cshp->chnp/dot_general | solution.py:134
  202.6 10.1 %while.26 = (s32[]{:T(128)}, f32[16,128,64]{2,1,0:T(8,128)S(1)}, f32[4,16,128,64]{3,2,1,0:T(8,128)}, f32[4,16]{1,0:T(4,128)S(1)}, f32[4,16,128,64]{3,2,1,0:T(8,128)}, /*index=5*/s32[]{:T(128)}, s32[]{:T(128)}) while((s32[]{:T(128)}, f32[16,128,64]{2,1,0:T(8,128)S(1)}, f32[4,16,128,64]{3,2,1,0:T(8,128)}, f32[4,16]{1,0:T(4,128)S(1)}, ...), condition=%wide.region_2.3_spmd.clone, body=%wide.region_1.2_spmd.clone.sunk | while | flops 524291 | bytes 3146528 | solution.py:136
  203.6 1.4 bitcast_add_fusion.2
  215.2 13.7 %all-reduce = bf16[128]{0:T(256)(128)(2,1)S(1)} all-reduce(bf16[128]{0:T(256)(128)(2,1)S(1)} %dynamic-update-slice), channel_id=3, replica_groups=mesh['ctx'=8,'inner'=4] {'ctx'}, use_global_device_ids=true, to_apply=%add | all-reduce | flops 128 | bytes 512
  230.0 3.3 %fusion.18 = f32[4,16,64,128]{3,2,1,0:T(8,128)} fusion(f32[16,4,128]{2,0,1:T(8,128)S(1)} %copy_bitcast_fusion.2, f32[16,4,128]{2,0,1:T(8,128)S(1)} %reduce_window_sum.22, f32[4,128,128]{2,1,0:T(8,128)S(1)} %fusion.65, pred[128,128]{1,0:T(8,128)(4,1)S(1)} %iota_compare_fusion, bf16[4,128,16,64]{1,0,3,2:T(4,128)(2,1)S(1)} %reshape.90), kind=kOutput, calls=%fused_computation.28 | convolution fusion | flops 139460608 | bytes 3489792 | tf_op jit(solution)/shard_map/hcts,cshp->cthp/dot_general | solution.py:130
  233.3 8.9 %all-gather.17.cloned.1.call-done = bf16[128,128,64]{1,2,0:T(8,128)(2,1)} async-done(((bf16[16,128,64]{1,2,0:T(8,128)(2,1)}), bf16[128,128,64]{1,2,0:T(8,128)(2,1)}) %all-gather.17.cloned.1.call-update) | async-done | bytes 2097168 | tf_op jit(solution)/shard_map/all_gather | solution.py:24
  242.3 11.0 %while.25 = (s32[]{:T(128)}, f32[16,128,64]{2,1,0:T(8,128)S(1)}, s32[]{:T(128)}, bf16[8,16]{1,0:T(8,128)(2,1)S(1)}, bf16[8,16,128,64]{2,3,1,0:T(8,128)(2,1)}, /*index=5*/s32[]{:T(128)}, s32[]{:T(128)}, s32[]{:T(128)}) while((s32[]{:T(128)}, f32[16,128,64]{2,1,0:T(8,128)S(1)}, s32[]{:T(128)}, bf16[8,16]{1,0:T(8,128)(2,1)S(1)}, ...), condition=%wide.region_6.7_spmd, body=%wide.region_5.6_spmd.sunk | while | flops 393237 | bytes 2359583 | solution.py:38
  253.3 5.2 %fusion.15 = f32[4,16,64,128]{3,2,1,0:T(8,128)S(1)} fusion(f32[4,16,128,64]{3,2,1,0:T(8,128)} %get-tuple-element.77, f32[16,4,128]{2,0,1:T(8,128)S(1)} %get-tuple-element.154, f32[4,128,128]{2,1,0:T(8,128)S(1)} %convert_element_type.135, f32[16,128,64]{2,1,0:T(8,128)S(1)} %get-tuple-element.79, f32[4,16]{1,0:T(4,128)S(1)} %exponential_bitcast_fusion.1), kind=kOutput, calls=%fused_computation.22 | convolution fusion | flops 139460608 | bytes 5013760 | tf_op jit(solution)/shard_map/hctn,chnp->cthp/dot_general | solution.py:149
  258.5 2.7 add_bitcast_fusion
  262.6 2.0 fusion.23
  265.0 16.9 %all_to_all.19 = bf16[4,128,1024]{1,2,0:T(8,128)(2,1)S(1)} all-to-all(bf16[4,128,1024]{1,2,0:T(8,128)(2,1)S(1)} %copy_bitcast_fusion.1), channel_id=1, replica_groups=mesh['ctx'=8,'inner'=4] {'inner'}, dimensions={0} | all-to-all | bytes 2097152 | tf_op jit(solution)/shard_map/all_to_all | solution.py:162
  (104 shorter events, 36.2 us)
Async XLA Ops:
  6.5 24.7 %all-gather.11.cloned.1.call-start = ((), (), s32[]{:S(2)}) async-start(), calls=%async_computation.2 | async-start | bytes 1179648 | tf_op jit(solution)/shard_map/all_gather | solution.py:84
  7.3 105.9 %all-gather.9.cloned.1.call-start = ((), (), s32[]{:S(2)}) async-start(), calls=%async_computation.1 | async-start | bytes 9437184 | tf_op jit(solution)/shard_map/all_gather | solution.py:83
  8.0 142.9 %all-gather.13.cloned.1.call-start = ((), (), s32[]{:S(2)}) async-start(), calls=%async_computation.3 | async-start | bytes 2621440 | tf_op jit(solution)/shard_map/all_gather | solution.py:102
  8.7 186.9 %all-gather.15.cloned.1.call-start = ((), (), s32[]{:S(2)}) async-start(), calls=%async_computation.4 | async-start | bytes 1310720 | tf_op jit(solution)/shard_map/all_gather | solution.py:117
  160.7 11.4 %copy-start.1 = (bf16[512,2320]{0,1:T(8,128)(2,1)}, bf16[512,2320]{0,1:T(8,128)(2,1)S(1)}, u32[]{:S(2)}) copy-start(bf16[512,2320]{0,1:T(8,128)(2,1)S(1)} %fusion.11) | copy-start | bytes 7127044
  160.7 7.3 %copy-start.5 = (f32[16]{0:T(128)S(1)}, f32[16]{0:T(128)}, u32[]{:S(2)}) copy-start(f32[16]{0:T(128)} %param.20) | copy-start | bytes 196
  160.8 7.3 %copy-start.3 = (f32[5,1024]{1,0:T(8,128)S(1)}, f32[5,1024]{1,0:T(8,128)}, u32[]{:S(2)}) copy-start(f32[5,1024]{1,0:T(8,128)} %param.17) | copy-start | bytes 61444
  160.8 9.7 %copy-start.4 = (f32[16]{0:T(128)S(1)}, f32[16]{0:T(128)}, u32[]{:S(2)}) copy-start(f32[16]{0:T(128)} %param.19) | copy-start | bytes 196
  161.0 4.6 %collective-permute-start.1 = (bf16[3,2,128]{2,0,1:T(4,128)(2,1)S(1)}, bf16[3,2,128]{2,0,1:T(4,128)(2,1)S(1)}, u32[]{:S(2)}, u32[]{:S(2)}) collective-permute-start(bf16[3,2,128]{2,0,1:T(4,128)(2,1)S(1)} %copy.64), channel_id=1, source_target_pairs={{0,4},{4,8},{8,12},{12,16},{16,20},{20,24},{24,28},{1,5},{5,9},{9,... | collective-permute-start | bytes 4616 | tf_op jit(solution)/shard_map/ppermute | solution.py:18
  168.0 74.2 %all-gather.17.cloned.1.call-start = ((), (), s32[]{:S(2)}) async-start(), calls=%async_computation.5 | async-start | bytes 2359296 | tf_op jit(solution)/shard_map/all_gather | solution.py:24
  169.0 4.7 %collective-permute-start = (bf16[3,1024]{0,1:T(8,128)(2,1)}, bf16[3,1024]{0,1:T(8,128)(2,1)}, u32[]{:S(2)}, u32[]{:S(2)}) collective-permute-start(bf16[3,1024]{0,1:T(8,128)(2,1)} %slice.106), channel_id=1, source_target_pairs={{0,4},{4,8},{8,12},{12,16},{16,20},{20,24},{24,28},{1,5},{5,9},{9,... | collective-permute-start | bytes 18440 | tf_op jit(solution)/shard_map/ppermute | solution.py:18
  202.6 11.1 %copy-start.6 = (u32[32]{0:T(128)S(1)}, u32[32]{0:T(128)}, u32[]{:S(2)}) copy-start(u32[32]{0:T(128)} %constant.96) | copy-start | bytes 388
  253.3 5.3 %copy-start = (f32[4,16,128,64]{3,2,1,0:T(8,128)S(1)}, f32[4,16,128,64]{3,2,1,0:T(8,128)}, u32[]{:S(2)}) copy-start(f32[4,16,128,64]{3,2,1,0:T(8,128)} %get-tuple-element.77) | copy-start | bytes 6291460
  253.3 5.3 %copy-start.2 = (f32[4,16,64,128]{3,2,1,0:T(8,128)S(1)}, f32[4,16,64,128]{3,2,1,0:T(8,128)}, u32[]{:S(2)}) copy-start(f32[4,16,64,128]{3,2,1,0:T(8,128)} %fusion.18) | copy-start | bytes 6291460
  262.6 2.0 dynamic-slice-start
Sparse Core Ops, SparseCore 0:
  8.9 22.2 all-gather.10
  32.8 80.3 all-gather.8
  115.0 35.8 all-gather.12
  168.1 27.4 all-gather.14
  213.8 28.3 all-gather.16
